TPU v7x, 32 devices: a whole 2x2x4 slice. The times are simulated.
32 devices in a mesh: groups: 2 (over y), hid: 8 (over z, x), row: 2 (over core).
Axes of the slice: x: 2, y: 2, z: 4, core: 2. Of those that a mesh axis runs over, the one named last changes fastest.
Arguments:
- gate_proj: bfloat16 [32, 32768], P(('groups', 'row'), 'hid'), parts along dimension 0, may hold values from -6 to 6
- up_proj: bfloat16 [32, 32768], P(('groups', 'row'), 'hid'), parts along dimension 0, may hold values from -6 to 6
- hadamard_signs: int32 [32768], P('hid'), may hold values from 0 to 1
- down_codes: bfloat16 [32768, 8192], P('hid', 'row'), may hold values from -127 to 127, as said below
- down_scales: int32 [8192], P('row'), may hold values from 128 to 1279
- residual: bfloat16 [32, 8192], P(('groups', 'hid'), 'row'), parts along dimension 0, may hold values from -16 to 16
- norm_gain: bfloat16 [8192], P('row'), may hold values from 0.099609375 to 1.8984375
- qkv_codes: bfloat16 [8192, 18432], P('row', 'hid'), may hold values from -127 to 127, as said below
- qkv_scales: int32 [18432], P('hid'), may hold values from 128 to 1279
Outputs:
- new_stream: bfloat16 [32, 8192], P(('groups', 'hid'), 'row'), parts along dimension 0
- joined_qkv: bfloat16 [32, 18432], P(('groups', 'row'), 'hid'), parts along dimension 0
There are 2 independent parts, one for each index of `groups`. A program takes and returns all parts, laid end to end along the dimension named above; an argument that names none is the same for every part. Nothing has to cross between parts.
Inputs may be any that keep to these rules, and one draw needn't show every extreme that they name: `down_codes`: every entry is a whole number. `qkv_codes`: every entry is a whole number.
All inputs are finite; a program needn't handle non-finite values.
Results may differ from a plain program's by a relative error of at most 0.0062.
Values may be sent and summed in bfloat16 or wider, within the bound.
A program may use at most 128 MiB of HBM per device.

v0:
```python
import functools
import math

import jax
import jax.numpy as jnp
from jax import lax
from jax.experimental import pallas as pl
from jax.experimental.pallas import tpu as pltpu
from jax.sharding import PartitionSpec as P

epsilon = 1e-05
F32 = jnp.float32
BF16 = jnp.bfloat16
MESH = pl.DeviceIdType.MESH


def each(count, step, start=0):
    if count - start <= 16:
        for index in range(start, count):
            step(index)
    else:

        def looped(index, carry):
            step(index)
            return carry

        lax.fori_loop(start, count, looped, 0)


def loop(count, step):
    def looped(index, carry):
        step(index)
        return carry

    lax.fori_loop(0, count, looped, 0)


def sylvester(order):
    both = lax.broadcasted_iota(jnp.int32, (order, order), 0) & lax.broadcasted_iota(
        jnp.int32, (order, order), 1
    )
    shift = 1
    while shift < order.bit_length():
        shift *= 2
    while shift > 1:
        shift //= 2
        both = both ^ lax.shift_right_logical(both, shift)
    return (1 - 2 * (both & 1)).astype(F32).astype(BF16)


def tile_of(width, largest):
    tile = largest // 128 * 128
    while width % tile:
        tile -= 128
    return tile


def kernel(
    A, B, J, width_total,
    gate_h, up_h, signs_h, wd_h, dscale_h, res_h, gain_h, wq_h, qscale_h,
    ns_o, out_o,
    gate, up, signs, dscale, res, gain1, qscale, wd, wq, gain,
    send1, recv1, xf, send2, recv2, lhsf, lhs, send3, recv3, send4, recv4, rowsf, lhs2, sq, proj,
    send5, recv5,
    in_sem, wd_sem, wq_sem, s1, r1, s2, r2, s3, r3, s4, r4, s5, r5,
):
    h = lax.axis_index("hid")
    r = lax.axis_index("row")
    N = A * B
    me = h * B + r
    Rl, FFl = gate.shape
    q = Rl // A
    R = Rl * B
    S = R // A
    C = wd.shape[2]
    Q = wq.shape[2]

    small = [
        pltpu.make_async_copy(src, dst, in_sem.at[k])
        for k, (src, dst) in enumerate(
            [(gate_h, gate), (up_h, up), (signs_h, signs), (dscale_h, dscale), (res_h, res),
             (gain_h, gain1), (qscale_h, qscale)]
        )
    ]
    for copy in small:
        copy.start()

    def wd_copy(j):
        return pltpu.make_async_copy(
            wd_h.at[:, pl.ds(pl.multiple_of(j * C, C), C)], wd.at[j], wd_sem.at[j]
        )

    def wq_copy(j):
        return pltpu.make_async_copy(
            wq_h.at[pl.ds(pl.multiple_of(j * C, C), C), :], wq.at[j], wq_sem.at[j]
        )

    for j in range(J):
        wd_copy(j).start(priority=1)

    barrier = pltpu.get_barrier_semaphore()

    def greet(t):
        peer = lax.rem(me + t, N)
        pl.semaphore_signal(
            barrier, inc=1, device_id={"hid": lax.div(peer, B), "row": lax.rem(peer, B)},
            device_id_type=MESH,
        )

    each(N, greet, 1)

    for copy in small[:3]:
        copy.wait()
    v = gate[...].astype(F32)
    hidden = (v / (1.0 + jnp.exp(-v)) * up[...].astype(F32)).astype(BF16).astype(F32)
    signed = hidden * (1 - 2 * signs[...]).astype(F32)
    for a in range(A):
        send1[a] = signed[a * q:(a + 1) * q, :].astype(BF16)
    recv1[h] = send1[h]
    pl.semaphore_wait(barrier, N - 1)

    def copy1(t):
        d = lax.rem(h + t, A)
        return pltpu.make_async_remote_copy(
            src_ref=send1.at[d], dst_ref=recv1.at[h], send_sem=s1.at[t - 1], recv_sem=r1.at[t - 1],
            device_id={"hid": d}, device_id_type=MESH,
        )

    each(A, lambda t: copy1(t).start(), 1)
    W = 256
    pieces = FFl // W
    order_right = sylvester(W)
    order_left = sylvester(A * pieces)
    for copy in small[3:]:
        copy.wait()
    gain[...] = gain1[...].astype(F32).reshape(1, -1)
    each(A, lambda t: copy1(t).wait(), 1)

    for k in range(q):
        for a in range(A):
            xf[a:a + 1, :] = recv1[a, k:k + 1, :].astype(F32)
        stacked = jnp.concatenate(
            [xf[:, p * W:(p + 1) * W] for p in range(pieces)], axis=0
        ).astype(BF16)
        right = jnp.dot(stacked, order_right, preferred_element_type=F32)
        top = right.astype(BF16)
        rest = right - top.astype(F32)
        middle = rest.astype(BF16)
        low = (rest - middle.astype(F32)).astype(BF16)
        both = (
            jnp.dot(order_left, low, preferred_element_type=F32)
            + jnp.dot(order_left, middle, preferred_element_type=F32)
        ) + jnp.dot(order_left, top, preferred_element_type=F32)
        both = both * (1.0 / math.sqrt(FFl * A))
        for p in range(pieces):
            xf[:, p * W:(p + 1) * W] = both[p * A:(p + 1) * A, :]
        for a in range(A):
            send2[a, k:k + 1, :] = xf[a:a + 1, :].astype(BF16)
    recv2[me] = send2[h]

    def copy2(t):
        peer = lax.rem(me + t, N)
        d = lax.div(peer, B)
        return pltpu.make_async_remote_copy(
            src_ref=send2.at[d], dst_ref=recv2.at[me], send_sem=s2.at[t - 1],
            recv_sem=r2.at[t - 1], device_id={"hid": d, "row": lax.rem(peer, B)},
            device_id_type=MESH,
        )

    each(N, lambda t: copy2(t).start(), 1)
    each(N, lambda t: copy2(t).wait(), 1)

    for j in range(J):
        wq_copy(j).start(priority=1)
    for b in range(B):
        for a in range(A):
            row = b * Rl + a * q
            lhsf[row:row + q, :] = recv2[a * B + b].astype(F32)
    lhs[...] = lhsf[...].astype(BF16)

    def copy3(t, j):
        d = lax.rem(h + t, A)
        return pltpu.make_async_remote_copy(
            src_ref=send3.at[j, d], dst_ref=recv3.at[j, h], send_sem=s3.at[t - 1, j],
            recv_sem=r3.at[t - 1, j], device_id={"hid": d}, device_id_type=MESH,
        )

    def copy4(t, j):
        d = lax.rem(h + t, A)
        return pltpu.make_async_remote_copy(
            src_ref=send4.at[j], dst_ref=recv4.at[j, h], send_sem=s4.at[t - 1, j],
            recv_sem=r4.at[t - 1, j], device_id={"hid": d}, device_id_type=MESH,
        )

    tile = tile_of(C, 512)

    def down_step(j):
        wd_copy(j).wait()
        for n in range(0, C, tile):
            part = jnp.dot(lhs[...], wd[j, :, n:n + tile], preferred_element_type=F32)
            for a in range(A):
                send3[j, a, :, n:n + tile] = part[a * S:(a + 1) * S, :].astype(BF16)
        recv3[j, h] = send3[j, h]
        each(A, lambda t: copy3(t, j).start(), 1)

    loop(J, down_step)

    def stream_step(j):
        each(A, lambda t: copy3(t, j).wait(), 1)
        total = recv3[j, 0].astype(F32)
        for a in range(1, A):
            total = total + recv3[j, a].astype(F32)
        columns = pl.ds(pl.multiple_of(j * C, C), C)
        total = total * (dscale[:, columns].astype(F32) * 2.0 ** (-23))
        stream = (res[:, columns].astype(F32) + total).astype(BF16)
        ns_o[:, columns] = stream
        send4[j] = stream
        recv4[j, h] = stream
        each(A, lambda t: copy4(t, j).start(), 1)

    loop(J, stream_step)

    sq[...] = jnp.zeros_like(sq)
    proj[...] = jnp.zeros_like(proj)
    tile_q = tile_of(Q, 768)

    def project_step(j):
        each(A, lambda t: copy4(t, j).wait(), 1)
        wq_copy(j).wait()
        for a in range(A):
            rowsf[a * S:(a + 1) * S, :] = recv4[j, a].astype(F32)
        wide = rowsf[...]
        columns = pl.ds(pl.multiple_of(j * C, C), C)
        lhs2[...] = (wide * gain[:, columns]).astype(BF16)
        sq[...] += jnp.sum(wide * wide, axis=1, keepdims=True)
        for n in range(0, Q, tile_q):
            proj[:, n:n + tile_q] += jnp.dot(
                lhs2[...], wq[j, :, n:n + tile_q], preferred_element_type=F32
            )

    loop(J, project_step)

    def copy5(t):
        d = lax.rem(r + t, B)
        return pltpu.make_async_remote_copy(
            src_ref=send5.at[d], dst_ref=recv5.at[r], send_sem=s5.at[t - 1],
            recv_sem=r5.at[t - 1], device_id={"row": d}, device_id_type=MESH,
        )

    for b in range(B):
        send5[b, :, :Q] = proj[b * Rl:(b + 1) * Rl, :]
        send5[b, :, Q:] = sq[b * Rl:(b + 1) * Rl, :]
    each(B, lambda t: copy5(t).start(), 1)
    recv5[r] = send5[r]
    each(B, lambda t: copy5(t).wait(), 1)
    total = recv5[0]
    for b in range(1, B):
        total = total + recv5[b]
    inverse = lax.rsqrt(total[:, Q:Q + 1] / width_total + epsilon)
    out_o[...] = (
        total[:, :Q] * inverse * (qscale[...].astype(F32).reshape(1, Q) * 2.0 ** (-22))
    ).astype(BF16)


def hand_over(ns, out, ns_o, out_o, sem):
    first = pltpu.make_async_copy(ns, ns_o, sem.at[0])
    second = pltpu.make_async_copy(out, out_o, sem.at[1])
    first.start()
    second.start()
    first.wait()
    second.wait()


def body(gate, up, signs, wd, dscale, res, gain, wq, qscale):
    A = lax.axis_size("hid")
    B = lax.axis_size("row")
    N = A * B
    Rl, FFl = gate.shape
    Dl = wd.shape[1]
    Q = wq.shape[1]
    R = Rl * B
    S = res.shape[0]
    q = Rl // A
    J = 4
    C = Dl // J
    any_spec = pl.BlockSpec(memory_space=pl.ANY)
    vmem_spec = pl.BlockSpec(memory_space=pltpu.VMEM)
    dma = pltpu.SemaphoreType.DMA
    call = pl.pallas_call(
        functools.partial(kernel, A, B, J, Dl * B),
        out_shape=(
            jax.ShapeDtypeStruct((S, Dl), BF16),
            jax.ShapeDtypeStruct((Rl, Q), BF16),
        ),
        in_specs=[any_spec] * 9,
        out_specs=(vmem_spec, vmem_spec),
        scratch_shapes=[
            pltpu.VMEM((Rl, FFl), BF16),
            pltpu.VMEM((Rl, FFl), BF16),
            pltpu.VMEM((1, FFl), jnp.int32),
            pltpu.VMEM((1, Dl), jnp.int32),
            pltpu.VMEM((S, Dl), BF16),
            pltpu.VMEM((Dl,), BF16),
            pltpu.VMEM((Q,), jnp.int32),
            pltpu.VMEM((J, FFl, C), BF16),
            pltpu.VMEM((J, C, Q), BF16),
            pltpu.VMEM((1, Dl), F32),
            pltpu.VMEM((A, q, FFl), BF16),
            pltpu.VMEM((A, q, FFl), BF16),
            pltpu.VMEM((A, FFl), F32),
            pltpu.VMEM((A, q, FFl), BF16),
            pltpu.VMEM((N, q, FFl), BF16),
            pltpu.VMEM((R, FFl), F32),
            pltpu.VMEM((R, FFl), BF16),
            pltpu.VMEM((J, A, S, C), BF16),
            pltpu.VMEM((J, A, S, C), BF16),
            pltpu.VMEM((J, S, C), BF16),
            pltpu.VMEM((J, A, S, C), BF16),
            pltpu.VMEM((R, C), F32),
            pltpu.VMEM((R, C), BF16),
            pltpu.VMEM((R, 128), F32),
            pltpu.VMEM((R, Q), F32),
            pltpu.VMEM((B, Rl, Q + 128), F32),
            pltpu.VMEM((B, Rl, Q + 128), F32),
            dma((7,)),
            dma((J,)),
            dma((J,)),
            dma((A - 1,)),
            dma((A - 1,)),
            dma((N - 1,)),
            dma((N - 1,)),
            dma((A - 1, J)),
            dma((A - 1, J)),
            dma((A - 1, J)),
            dma((A - 1, J)),
            dma((B - 1,)),
            dma((B - 1,)),
        ],
        compiler_params=pltpu.CompilerParams(
            collective_id=0, has_side_effects=True, vmem_limit_bytes=63 * 1024 * 1024
        ),
    )
    made = call(
        gate, up, signs.reshape(1, -1), wd, dscale.reshape(1, -1), res, gain, wq,
        qscale,
    )
    return pl.pallas_call(
        hand_over,
        out_shape=(jax.ShapeDtypeStruct((S, Dl), BF16), jax.ShapeDtypeStruct((Rl, Q), BF16)),
        in_specs=[vmem_spec, vmem_spec],
        out_specs=(any_spec, any_spec),
        scratch_shapes=[dma((2,))],
    )(*made)


def solution(mesh):
    return jax.shard_map(
        body,
        mesh=mesh,
        in_specs=(
            P(("groups", "row"), "hid"),
            P(("groups", "row"), "hid"),
            P("hid"),
            P("hid", "row"),
            P("row"),
            P(("groups", "hid"), "row"),
            P("row"),
            P("row", "hid"),
            P("hid"),
        ),
        out_specs=(P(("groups", "hid"), "row"), P(("groups", "row"), "hid")),
        check_vma=False,
    )
```

profile of v0, /device:TPU:0, one launch (start us, length us, event | category | flops | bytes accessed | tf_op | source)
XLA Modules:
  0.0 36.9 jit_solution(17271988377374057545)
XLA Ops:
  0.6 34.8 %shard_map.104 = (bf16[2,4096]{1,0:T(2,128)(2,1)}, bf16[8,2304]{1,0:T(8,128)(2,1)}) custom-call(bf16[8,4096]{1,0:T(8,128)(2,1)} %gate_h.1, bf16[8,4096]{1,0:T(8,128)(2,1)} %up_h.1, s32[1,4096]{1,0:T(1,128)} %bitcast.2, bf16[4096,4096]{1,0:T(8,128)(2,1)} %wd_h.1, s32[1,4096]{1,0:T(1,128)} %bitcast.3, bf16[2,4096]{1,0:T(2,128)(2,1)} %res_h.1, ...), custom_call_target="tpu_custom_call" | custom-call | tf_op jit(solution)/shard_map/pallas_call | solution.py:343
  35.5 1.4 %shard_map.105 = (bf16[2,4096]{1,0:T(2,128)(2,1)}, bf16[8,2304]{1,0:T(8,128)(2,1)}) custom-call(bf16[2,4096]{1,0:T(2,128)(2,1)} %get-tuple-element.4.ns, bf16[8,2304]{1,0:T(8,128)(2,1)} %get-tuple-element.5.out), custom_call_target="tpu_custom_call" | custom-call | tf_op jit(solution)/shard_map/pallas_call | solution.py:347
where the time goes:
time: 37.1 us; the launch traced here: 36.9 us
  Pallas kernels  36.3 us (98%)
  between operations  0.64 us (2%)
    pallas_call x1, Pallas kernels, body(): call(gate, up, signs.reshape(1, -1), wd, dscale.reshape(1, -1), res, gain...  34.8 us
    pallas_call x1, Pallas kernels, body(): pl.pallas_call(hand_over, out_shape=(jax.ShapeDtypeStruct((S, Dl), BF16),...  1.42 us

commit v1 on v0

v1 whole, which is shorter than its diff:
```python
import functools
import math

import jax
import jax.numpy as jnp
from jax import lax
from jax.experimental import pallas as pl
from jax.experimental.pallas import tpu as pltpu
from jax.sharding import PartitionSpec as P

epsilon = 1e-05
F32 = jnp.float32
BF16 = jnp.bfloat16
MESH = pl.DeviceIdType.MESH


def each(count, step, start=0):
    if count - start <= 16:
        for index in range(start, count):
            step(index)
    else:

        def looped(index, carry):
            step(index)
            return carry

        lax.fori_loop(start, count, looped, 0)


def loop(count, step):
    def looped(index, carry):
        step(index)
        return carry

    lax.fori_loop(0, count, looped, 0)


def sylvester(order):
    both = lax.broadcasted_iota(jnp.int32, (order, order), 0) & lax.broadcasted_iota(
        jnp.int32, (order, order), 1
    )
    shift = 1
    while shift < order.bit_length():
        shift *= 2
    while shift > 1:
        shift //= 2
        both = both ^ lax.shift_right_logical(both, shift)
    return (1 - 2 * (both & 1)).astype(F32).astype(BF16)


def tile_of(width, largest):
    tile = largest // 128 * 128
    while width % tile:
        tile -= 128
    return tile


def butterfly(parts):
    step = 1
    while step < len(parts):
        parts = [
            parts[i] + parts[i + step] if i & step == 0 else parts[i - step] - parts[i]
            for i in range(len(parts))
        ]
        step *= 2
    return parts


def kernel(
    A, B, J, M, lo, width_total,
    gate_h, up_h, signs_h, wd_h, dscale_h, res_h, gain_h, wq_h, qscale_h,
    ns_o, out_o,
    gate, up, signs, dscale, res, gain1, qscale, wd, wq, gain,
    send1, recv1, recvr, resf, send2, recv2, lhsf, lhs, send3, recv3, send4, recv4, rowsf, lhs2,
    sq, proj, send5, recv5,
    in_sem, wd_sem, wq_sem, s1, r1, sr, rr, s2, r2, s3, r3, s4, r4, s5, r5,
):
    h = lax.axis_index("hid")
    r = lax.axis_index("row")
    N = A * B
    me = h * B + r
    mine = h - lo
    owner = (h >= lo) & (h < lo + M)
    Rl, FFl = gate.shape
    q = Rl // M
    R = Rl * B
    S = res.shape[0]
    T = R // M
    G = A // M
    C = wd.shape[2]
    Q = wq.shape[2]

    small = [
        pltpu.make_async_copy(src, dst, in_sem.at[k])
        for k, (src, dst) in enumerate(
            [(gate_h, gate), (up_h, up), (signs_h, signs), (res_h, res), (dscale_h, dscale),
             (gain_h, gain1), (qscale_h, qscale)]
        )
    ]
    for copy in small:
        copy.start()

    def wd_copy(j):
        return pltpu.make_async_copy(
            wd_h.at[:, pl.ds(pl.multiple_of(j * C, C), C)], wd.at[j], wd_sem.at[j]
        )

    def wq_copy(j):
        return pltpu.make_async_copy(
            wq_h.at[pl.ds(pl.multiple_of(j * C, C), C), :], wq.at[j], wq_sem.at[j]
        )

    for j in range(J):
        wd_copy(j).start(priority=1)

    barrier = pltpu.get_barrier_semaphore()

    def greet(t):
        peer = lax.rem(me + t, N)
        d = lax.div(peer, B)

        @pl.when(owner | ((d >= lo) & (d < lo + M)) | (d == h))
        def _():
            pl.semaphore_signal(
                barrier, inc=1, device_id={"hid": d, "row": lax.rem(peer, B)}, device_id_type=MESH
            )

    each(N, greet, 1)

    def but_mine(count, first, step):
        def guarded(index):
            @pl.when(first + index != h)
            def _():
                step(index)

        each(count, guarded)

    W = 256
    pieces = FFl // W
    order = sylvester(W)
    for copy in small[:3]:
        copy.wait()
    v = gate[...].astype(F32)
    hidden = (v / (1.0 + jnp.exp(-v)) * up[...].astype(F32)).astype(BF16).astype(F32)
    signed = hidden * (1 - 2 * signs[...]).astype(F32)
    stacked = jnp.concatenate(
        [signed[:, p * W:(p + 1) * W] for p in range(pieces)], axis=0
    ).astype(BF16)
    right = jnp.dot(stacked, order, preferred_element_type=F32)
    parts = butterfly([right[p * Rl:(p + 1) * Rl, :] for p in range(pieces)])
    for p in range(pieces):
        for m in range(M):
            send1[m, :, p * W:(p + 1) * W] = parts[p][m * q:(m + 1) * q, :].astype(BF16)

    @pl.when(owner)
    def _():
        recv1[h] = send1[mine]

    small[3].wait()

    @pl.when(owner)
    def _():
        pl.semaphore_wait(barrier, N - 1)

    @pl.when(jnp.logical_not(owner))
    def _():
        pl.semaphore_wait(barrier, M * B + B - 1)

    def copy1(m, a):
        return pltpu.make_async_remote_copy(
            src_ref=send1.at[m], dst_ref=recv1.at[a], send_sem=s1.at[m], recv_sem=r1.at[a],
            device_id={"hid": lo + m}, device_id_type=MESH,
        )

    home = lo + lax.div(h, G)

    def copyr(g):
        return pltpu.make_async_remote_copy(
            src_ref=res, dst_ref=recvr.at[g], send_sem=sr.at[0], recv_sem=rr.at[g],
            device_id={"hid": home}, device_id_type=MESH,
        )

    but_mine(M, lo, lambda m: copy1(m, h).start())

    @pl.when(home != h)
    def _():
        copyr(lax.rem(h, G)).start()

    @pl.when(home == h)
    def _():
        recvr[lax.rem(h, G)] = res[...]

    for copy in small[4:]:
        copy.wait()
    gain[...] = gain1[...].astype(F32).reshape(1, -1)

    def copy2(t):
        peer = lax.rem(me + t, N)
        d = lax.div(peer, B)
        return pltpu.make_async_remote_copy(
            src_ref=send2.at[d], dst_ref=recv2.at[mine * B + r], send_sem=s2.at[t - 1],
            recv_sem=r2.at[mine * B + r], device_id={"hid": d, "row": lax.rem(peer, B)},
            device_id_type=MESH,
        )

    def wait2(k):
        @pl.when(lo * B + k != me)
        def _():
            pltpu.make_async_remote_copy(
                src_ref=send2.at[0], dst_ref=recv2.at[k], send_sem=s2.at[0], recv_sem=r2.at[k],
                device_id={"hid": h}, device_id_type=MESH,
            ).wait_recv()

    @pl.when(owner)
    def _():
        but_mine(A, 0, lambda a: copy1(0, a).wait_recv())
        V = min(FFl, 512)
        for c in range(0, FFl, V):
            mixed = butterfly([recv1[a, :, c:c + V].astype(F32) for a in range(A)])
            for a in range(A):
                send2[a, :, c:c + V] = (mixed[a] * (1.0 / math.sqrt(FFl * A))).astype(BF16)
        each(N, lambda t: copy2(t).start(), 1)
        recv2[mine * B + r] = send2[h]

    each(M * B, wait2)

    for j in range(J):
        wq_copy(j).start(priority=1)
    for b in range(B):
        for m in range(M):
            row = b * Rl + m * q
            lhsf[row:row + q, :] = recv2[m * B + b].astype(F32)
    lhs[...] = lhsf[...].astype(BF16)

    def copy3(m, a, j):
        return pltpu.make_async_remote_copy(
            src_ref=send3.at[j, m], dst_ref=recv3.at[j, a], send_sem=s3.at[m, j],
            recv_sem=r3.at[a, j], device_id={"hid": lo + m}, device_id_type=MESH,
        )

    def copy4(t, m, j):
        d = lax.rem(h + t, A)
        return pltpu.make_async_remote_copy(
            src_ref=send4.at[j], dst_ref=recv4.at[j, m], send_sem=s4.at[t - 1, j],
            recv_sem=r4.at[m, j], device_id={"hid": d}, device_id_type=MESH,
        )

    tile = tile_of(C, 512)

    def down_step(j):
        wd_copy(j).wait()
        for n in range(0, C, tile):
            part = jnp.dot(lhs[...], wd[j, :, n:n + tile], preferred_element_type=F32)
            for m in range(M):
                send3[j, m, :, n:n + tile] = part[m * T:(m + 1) * T, :].astype(BF16)

        but_mine(M, lo, lambda m: copy3(m, h, j).start())

        @pl.when(owner)
        def _():
            recv3[j, h] = send3[j, mine]

    loop(J, down_step)

    def stream_step(j):
        but_mine(A, 0, lambda a: copy3(0, a, j).wait_recv())
        total = recv3[j, 0].astype(F32)
        for a in range(1, A):
            total = total + recv3[j, a].astype(F32)
        columns = pl.ds(pl.multiple_of(j * C, C), C)
        total = total * (dscale[:, columns].astype(F32) * 2.0 ** (-23))
        stream = (resf[:, columns] + total).astype(BF16)
        send4[j] = stream
        recv4[j, mine] = stream
        each(A, lambda t: copy4(t, mine, j).start(), 1)

    @pl.when(owner)
    def _():
        for g in range(G):
            @pl.when(mine * G + g != h)
            def _(g=g):
                copyr(g).wait_recv()
        for g in range(G):
            resf[g * S:(g + 1) * S, :] = recvr[g].astype(F32)
        loop(J, stream_step)

    sq[...] = jnp.zeros_like(sq)
    proj[...] = jnp.zeros_like(proj)
    tile_q = tile_of(Q, 768)

    def project_step(j):
        but_mine(M, lo, lambda m: copy4(1, m, j).wait_recv())
        wq_copy(j).wait()
        for m in range(M):
            rowsf[m * T:(m + 1) * T, :] = recv4[j, m].astype(F32)
        wide = rowsf[...]
        columns = pl.ds(pl.multiple_of(j * C, C), C)
        for a in range(A):
            @pl.when(h == a)
            def _():
                ns_o[:, columns] = rowsf[a * S:(a + 1) * S, :].astype(BF16)
        lhs2[...] = (wide * gain[:, columns]).astype(BF16)
        sq[...] += jnp.sum(wide * wide, axis=1, keepdims=True)
        for n in range(0, Q, tile_q):
            proj[:, n:n + tile_q] += jnp.dot(
                lhs2[...], wq[j, :, n:n + tile_q], preferred_element_type=F32
            )

    loop(J, project_step)

    def copy5(t):
        d = lax.rem(r + t, B)
        return pltpu.make_async_remote_copy(
            src_ref=send5.at[d], dst_ref=recv5.at[r], send_sem=s5.at[t - 1],
            recv_sem=r5.at[t - 1], device_id={"row": d}, device_id_type=MESH,
        )

    for b in range(B):
        send5[b, :, :Q] = proj[b * Rl:(b + 1) * Rl, :]
        send5[b, :, Q:] = sq[b * Rl:(b + 1) * Rl, :]
    each(B, lambda t: copy5(t).start(), 1)
    recv5[r] = send5[r]

    but_mine(M, lo, lambda m: copy1(m, h).wait_send())

    @pl.when(home != h)
    def _():
        copyr(0).wait_send()

    for j in range(J):
        but_mine(M, lo, lambda m, j=j: copy3(m, h, j).wait_send())

    @pl.when(owner)
    def _():
        each(N, lambda t: copy2(t).wait_send(), 1)
        for j in range(J):
            each(A, lambda t, j=j: copy4(t, mine, j).wait_send(), 1)

    each(B, lambda t: copy5(t).wait(), 1)
    total = recv5[0]
    for b in range(1, B):
        total = total + recv5[b]
    inverse = lax.rsqrt(total[:, Q:Q + 1] / width_total + epsilon)
    out_o[...] = (
        total[:, :Q] * inverse * (qscale[...].astype(F32).reshape(1, Q) * 2.0 ** (-22))
    ).astype(BF16)


def hand_over(ns, out, ns_o, out_o, sem):
    first = pltpu.make_async_copy(ns, ns_o, sem.at[0])
    second = pltpu.make_async_copy(out, out_o, sem.at[1])
    first.start()
    second.start()
    first.wait()
    second.wait()


def body(gate, up, signs, wd, dscale, res, gain, wq, qscale):
    A = lax.axis_size("hid")
    B = lax.axis_size("row")
    N = A * B
    M = A // 2
    lo = (A - M) // 2
    Rl, FFl = gate.shape
    Dl = wd.shape[1]
    Q = wq.shape[1]
    R = Rl * B
    S = res.shape[0]
    q = Rl // M
    T = R // M
    J = 4
    C = Dl // J
    any_spec = pl.BlockSpec(memory_space=pl.ANY)
    vmem_spec = pl.BlockSpec(memory_space=pltpu.VMEM)
    dma = pltpu.SemaphoreType.DMA
    call = pl.pallas_call(
        functools.partial(kernel, A, B, J, M, lo, Dl * B),
        out_shape=(pltpu.VMEM((S, Dl), BF16), pltpu.VMEM((Rl, Q), BF16)),
        in_specs=[any_spec] * 9,
        out_specs=(vmem_spec, vmem_spec),
        scratch_shapes=[
            pltpu.VMEM((Rl, FFl), BF16),
            pltpu.VMEM((Rl, FFl), BF16),
            pltpu.VMEM((1, FFl), jnp.int32),
            pltpu.VMEM((1, Dl), jnp.int32),
            pltpu.VMEM((S, Dl), BF16),
            pltpu.VMEM((Dl,), BF16),
            pltpu.VMEM((Q,), jnp.int32),
            pltpu.VMEM((J, FFl, C), BF16),
            pltpu.VMEM((J, C, Q), BF16),
            pltpu.VMEM((1, Dl), F32),
            pltpu.VMEM((M, q, FFl), BF16),
            pltpu.VMEM((A, q, FFl), BF16),
            pltpu.VMEM((A // M, S, Dl), BF16),
            pltpu.VMEM((T, Dl), F32),
            pltpu.VMEM((A, q, FFl), BF16),
            pltpu.VMEM((M * B, q, FFl), BF16),
            pltpu.VMEM((R, FFl), F32),
            pltpu.VMEM((R, FFl), BF16),
            pltpu.VMEM((J, M, T, C), BF16),
            pltpu.VMEM((J, A, T, C), BF16),
            pltpu.VMEM((J, T, C), BF16),
            pltpu.VMEM((J, M, T, C), BF16),
            pltpu.VMEM((R, C), F32),
            pltpu.VMEM((R, C), BF16),
            pltpu.VMEM((R, 128), F32),
            pltpu.VMEM((R, Q), F32),
            pltpu.VMEM((B, Rl, Q + 128), F32),
            pltpu.VMEM((B, Rl, Q + 128), F32),
            dma((7,)),
            dma((J,)),
            dma((J,)),
            dma((M,)),
            dma((A,)),
            dma((1,)),
            dma((A // M,)),
            dma((N - 1,)),
            dma((M * B,)),
            dma((M, J)),
            dma((A, J)),
            dma((A - 1, J)),
            dma((M, J)),
            dma((B - 1,)),
            dma((B - 1,)),
        ],
        compiler_params=pltpu.CompilerParams(
            collective_id=0, has_side_effects=True, vmem_limit_bytes=62 * 1024 * 1024
        ),
    )
    made = call(
        gate, up, signs.reshape(1, -1), wd, dscale.reshape(1, -1), res, gain, wq,
        qscale,
    )
    return pl.pallas_call(
        hand_over,
        out_shape=(jax.ShapeDtypeStruct((S, Dl), BF16), jax.ShapeDtypeStruct((Rl, Q), BF16)),
        in_specs=[vmem_spec, vmem_spec],
        out_specs=(any_spec, any_spec),
        scratch_shapes=[dma((2,))],
    )(*(pltpu.with_memory_space_constraint(part, pltpu.VMEM) for part in made))


def solution(mesh):
    return jax.shard_map(
        body,
        mesh=mesh,
        in_specs=(
            P(("groups", "row"), "hid"),
            P(("groups", "row"), "hid"),
            P("hid"),
            P("hid", "row"),
            P("row"),
            P(("groups", "hid"), "row"),
            P("row"),
            P("row", "hid"),
            P("hid"),
        ),
        out_specs=(P(("groups", "hid"), "row"), P(("groups", "row"), "hid")),
        check_vma=False,
    )
```

time: 37.1 us -> 30.3 us (0.82)
  Pallas kernels: 36.3 us -> 29.5 us
    pallas_call x1, Pallas kernels: 34.8 us -> 28.9 us  [body(): call(gate, up, signs.reshape(1, -1), wd, dscale.reshape(1, -1), res, gain...]
    pallas_call x1, Pallas kernels: 1.42 us -> 0.64 us  [body(): pl.pallas_call(hand_over, out_shape=(jax.ShapeDtypeStruct((S, Dl), BF16),...]
where the time goes in v1:
time: 30.3 us; the launch traced here: 30.2 us
  Pallas kernels  29.5 us (97%)
  between operations  0.64 us (2%)
    pallas_call x1, Pallas kernels, body(): call(gate, up, signs.reshape(1, -1), wd, dscale.reshape(1, -1), res, gain...  28.9 us
    pallas_call x1, Pallas kernels, body(): pl.pallas_call(hand_over, out_shape=(jax.ShapeDtypeStruct((S, Dl), BF16),...  0.64 us

profile of v1, /device:TPU:0, one launch (start us, length us, event | category | flops | bytes accessed | tf_op | source)
XLA Modules:
  0.0 30.2 jit_solution(7734850883310202734)
XLA Ops:
  0.6 28.9 %shard_map.104 = (bf16[2,4096]{1,0:T(2,128)(2,1)S(1)}, bf16[8,2304]{1,0:T(8,128)(2,1)S(1)}) custom-call(bf16[8,4096]{1,0:T(8,128)(2,1)} %gate_h.1, bf16[8,4096]{1,0:T(8,128)(2,1)} %up_h.1, s32[1,4096]{1,0:T(1,128)} %bitcast.2, bf16[4096,4096]{1,0:T(8,128)(2,1)} %wd_h.1, s32[1,4096]{1,0:T(1,128)} %bitcast.3, bf16[2,4096]{1,0:T(2,128)(2,1)} %res_h.1, ...), custom_call_target="tpu_custom_call" | custom-call | tf_op jit(solution)/shard_map/pallas_call | solution.py:430
  29.5 0.6 %shard_map.105 = (bf16[2,4096]{1,0:T(2,128)(2,1)}, bf16[8,2304]{1,0:T(8,128)(2,1)}) custom-call(bf16[2,4096]{1,0:T(2,128)(2,1)S(1)} %get-tuple-element.4.ns, bf16[8,2304]{1,0:T(8,128)(2,1)S(1)} %get-tuple-element.5.out), custom_call_target="tpu_custom_call" | custom-call | tf_op jit(solution)/shard_map/pallas_call | solution.py:434

commit v2 on v1

--- a/solution.py
+++ b/solution.py
@@ -97,7 +97,23 @@
              (gain_h, gain1), (qscale_h, qscale)]
         )
     ]
-    for copy in small:
+    barrier = pltpu.get_barrier_semaphore()
+
+    def greet(t):
+        peer = lax.rem(me + t, N)
+        d = lax.div(peer, B)
+        e = lax.rem(peer, B)
+
+        @pl.when((owner & (((d >= lo) & (d < lo + M)) | (e == r))) | (d == h))
+        def _():
+            pl.semaphore_signal(
+                barrier, inc=1, device_id={"hid": d, "row": e}, device_id_type=MESH
+            )
+
+    for copy in small[:3]:
+        copy.start()
+    each(N, greet, 1)
+    for copy in small[3:]:
         copy.start()
 
     def wd_copy(j):
@@ -113,19 +129,17 @@
     for j in range(J):
         wd_copy(j).start(priority=1)
 
-    barrier = pltpu.get_barrier_semaphore()
-
-    def greet(t):
-        peer = lax.rem(me + t, N)
-        d = lax.div(peer, B)
-
-        @pl.when(owner | ((d >= lo) & (d < lo + M)) | (d == h))
+    def landed(part, sem):
+        pltpu.make_async_copy(part, part, sem).wait()
+
+    def all_landed(full, fewer, sem):
+        @pl.when(owner)
         def _():
-            pl.semaphore_signal(
-                barrier, inc=1, device_id={"hid": d, "row": lax.rem(peer, B)}, device_id_type=MESH
-            )
-
-    each(N, greet, 1)
+            landed(fewer, sem)
+
+        @pl.when(jnp.logical_not(owner))
+        def _():
+            landed(full, sem)
 
     def but_mine(count, first, step):
         def guarded(index):
@@ -160,15 +174,15 @@
 
     @pl.when(owner)
     def _():
-        pl.semaphore_wait(barrier, N - 1)
+        pl.semaphore_wait(barrier, M * B - 1)
 
     @pl.when(jnp.logical_not(owner))
     def _():
-        pl.semaphore_wait(barrier, M * B + B - 1)
+        pl.semaphore_wait(barrier, M + B - 1)
 
     def copy1(m, a):
         return pltpu.make_async_remote_copy(
-            src_ref=send1.at[m], dst_ref=recv1.at[a], send_sem=s1.at[m], recv_sem=r1.at[a],
+            src_ref=send1.at[m], dst_ref=recv1.at[a], send_sem=s1.at[0], recv_sem=r1.at[0],
             device_id={"hid": lo + m}, device_id_type=MESH,
         )
 
@@ -197,23 +211,16 @@
     def copy2(t):
         peer = lax.rem(me + t, N)
         d = lax.div(peer, B)
-        return pltpu.make_async_remote_copy(
-            src_ref=send2.at[d], dst_ref=recv2.at[mine * B + r], send_sem=s2.at[t - 1],
-            recv_sem=r2.at[mine * B + r], device_id={"hid": d, "row": lax.rem(peer, B)},
+        e = lax.rem(peer, B)
+        return pltpu.make_async_remote_copy(
+            src_ref=send2.at[d], dst_ref=recv2.at[mine * B + r], send_sem=s2.at[e],
+            recv_sem=r2.at[0], device_id={"hid": d, "row": e},
             device_id_type=MESH,
         )
 
-    def wait2(k):
-        @pl.when(lo * B + k != me)
-        def _():
-            pltpu.make_async_remote_copy(
-                src_ref=send2.at[0], dst_ref=recv2.at[k], send_sem=s2.at[0], recv_sem=r2.at[k],
-                device_id={"hid": h}, device_id_type=MESH,
-            ).wait_recv()
-
     @pl.when(owner)
     def _():
-        but_mine(A, 0, lambda a: copy1(0, a).wait_recv())
+        landed(recv1.at[pl.ds(0, A - 1)], r1.at[0])
         V = min(FFl, 512)
         for c in range(0, FFl, V):
             mixed = butterfly([recv1[a, :, c:c + V].astype(F32) for a in range(A)])
@@ -222,7 +229,7 @@
         each(N, lambda t: copy2(t).start(), 1)
         recv2[mine * B + r] = send2[h]
 
-    each(M * B, wait2)
+    all_landed(recv2, recv2.at[pl.ds(0, M * B - 1)], r2.at[0])
 
     for j in range(J):
         wq_copy(j).start(priority=1)
@@ -234,15 +241,15 @@
 
     def copy3(m, a, j):
         return pltpu.make_async_remote_copy(
-            src_ref=send3.at[j, m], dst_ref=recv3.at[j, a], send_sem=s3.at[m, j],
-            recv_sem=r3.at[a, j], device_id={"hid": lo + m}, device_id_type=MESH,
+            src_ref=send3.at[j, m], dst_ref=recv3.at[j, a], send_sem=s3.at[0],
+            recv_sem=r3.at[j], device_id={"hid": lo + m}, device_id_type=MESH,
         )
 
     def copy4(t, m, j):
         d = lax.rem(h + t, A)
         return pltpu.make_async_remote_copy(
-            src_ref=send4.at[j], dst_ref=recv4.at[j, m], send_sem=s4.at[t - 1, j],
-            recv_sem=r4.at[m, j], device_id={"hid": d}, device_id_type=MESH,
+            src_ref=send4.at[j], dst_ref=recv4.at[j, m], send_sem=s4.at[0],
+            recv_sem=r4.at[j], device_id={"hid": d}, device_id_type=MESH,
         )
 
     tile = tile_of(C, 512)
@@ -263,7 +270,7 @@
     loop(J, down_step)
 
     def stream_step(j):
-        but_mine(A, 0, lambda a: copy3(0, a, j).wait_recv())
+        landed(recv3.at[j, pl.ds(0, A - 1)], r3.at[j])
         total = recv3[j, 0].astype(F32)
         for a in range(1, A):
             total = total + recv3[j, a].astype(F32)
@@ -289,7 +296,7 @@
     tile_q = tile_of(Q, 768)
 
     def project_step(j):
-        but_mine(M, lo, lambda m: copy4(1, m, j).wait_recv())
+        all_landed(recv4.at[j], recv4.at[j, pl.ds(0, M - 1)], r4.at[j])
         wq_copy(j).wait()
         for m in range(M):
             rowsf[m * T:(m + 1) * T, :] = recv4[j, m].astype(F32)
@@ -321,20 +328,24 @@
     each(B, lambda t: copy5(t).start(), 1)
     recv5[r] = send5[r]
 
-    but_mine(M, lo, lambda m: copy1(m, h).wait_send())
+    all_landed(send1, send1.at[pl.ds(0, M - 1)], s1.at[0])
+    all_landed(send3, send3.at[:, pl.ds(0, M - 1)], s3.at[0])
 
     @pl.when(home != h)
     def _():
         copyr(0).wait_send()
 
-    for j in range(J):
-        but_mine(M, lo, lambda m, j=j: copy3(m, h, j).wait_send())
-
     @pl.when(owner)
     def _():
-        each(N, lambda t: copy2(t).wait_send(), 1)
-        for j in range(J):
-            each(A, lambda t, j=j: copy4(t, mine, j).wait_send(), 1)
+        landed(recv3.at[:, pl.ds(0, A - 1)], s4.at[0])
+        for e in range(B):
+            @pl.when(r == e)
+            def _(e=e):
+                landed(send2.at[pl.ds(0, A - 1)], s2.at[e])
+
+            @pl.when(r != e)
+            def _(e=e):
+                landed(send2, s2.at[e])
 
     each(B, lambda t: copy5(t).wait(), 1)
     total = recv5[0]
@@ -368,7 +379,7 @@
     S = res.shape[0]
     q = Rl // M
     T = R // M
-    J = 4
+    J = 8 if Dl % (8 * 128) == 0 else 4
     C = Dl // J
     any_spec = pl.BlockSpec(memory_space=pl.ANY)
     vmem_spec = pl.BlockSpec(memory_space=pltpu.VMEM)
@@ -410,16 +421,16 @@
             dma((7,)),
             dma((J,)),
             dma((J,)),
-            dma((M,)),
-            dma((A,)),
+            dma((1,)),
+            dma((1,)),
             dma((1,)),
             dma((A // M,)),
-            dma((N - 1,)),
-            dma((M * B,)),
-            dma((M, J)),
-            dma((A, J)),
-            dma((A - 1, J)),
-            dma((M, J)),
+            dma((B,)),
+            dma((1,)),
+            dma((1,)),
+            dma((J,)),
+            dma((1,)),
+            dma((J,)),
             dma((B - 1,)),
             dma((B - 1,)),
         ],

time: 30.3 us -> 29 us (0.957)
  Pallas kernels: 29.5 us -> 28.2 us
    pallas_call x1, Pallas kernels: 28.9 us -> 27.5 us  [body(): call(gate, up, signs.reshape(1, -1), wd, dscale.reshape(1, -1), res, gain...]
where the time goes in v2:
time: 29 us; the launch traced here: 28.8 us
  Pallas kernels  28.2 us (97%)
  between operations  0.64 us (2%)
    pallas_call x1, Pallas kernels, body(): call(gate, up, signs.reshape(1, -1), wd, dscale.reshape(1, -1), res, gain...  27.5 us
    pallas_call x1, Pallas kernels, body(): pl.pallas_call(hand_over, out_shape=(jax.ShapeDtypeStruct((S, Dl), BF16),...  0.64 us

profile of v2, /device:TPU:0, one launch (start us, length us, event | category | flops | bytes accessed | tf_op | source)
XLA Modules:
  0.0 28.8 jit_solution(17566878603985356865)
XLA Ops:
  0.6 27.5 %shard_map.104 = (bf16[2,4096]{1,0:T(2,128)(2,1)S(1)}, bf16[8,2304]{1,0:T(8,128)(2,1)S(1)}) custom-call(bf16[8,4096]{1,0:T(8,128)(2,1)} %gate_h.1, bf16[8,4096]{1,0:T(8,128)(2,1)} %up_h.1, s32[1,4096]{1,0:T(1,128)} %bitcast.2, bf16[4096,4096]{1,0:T(8,128)(2,1)} %wd_h.1, s32[1,4096]{1,0:T(1,128)} %bitcast.3, bf16[2,4096]{1,0:T(2,128)(2,1)} %res_h.1, ...), custom_call_target="tpu_custom_call" | custom-call | tf_op jit(solution)/shard_map/pallas_call | solution.py:441
  28.2 0.6 %shard_map.105 = (bf16[2,4096]{1,0:T(2,128)(2,1)}, bf16[8,2304]{1,0:T(8,128)(2,1)}) custom-call(bf16[2,4096]{1,0:T(2,128)(2,1)S(1)} %get-tuple-element.4.ns, bf16[8,2304]{1,0:T(8,128)(2,1)S(1)} %get-tuple-element.5.out), custom_call_target="tpu_custom_call" | custom-call | tf_op jit(solution)/shard_map/pallas_call | solution.py:445

commit v3 on v2

--- a/solution.py
+++ b/solution.py
@@ -27,12 +27,12 @@
         lax.fori_loop(start, count, looped, 0)
 
 
-def loop(count, step):
+def loop(count, step, start=0):
     def looped(index, carry):
         step(index)
         return carry
 
-    lax.fori_loop(0, count, looped, 0)
+    lax.fori_loop(start, count, looped, 0)
 
 
 def sylvester(order):
@@ -67,12 +67,12 @@
 
 
 def kernel(
-    A, B, J, M, lo, width_total,
+    A, B, J, KC, E, M, lo, width_total,
     gate_h, up_h, signs_h, wd_h, dscale_h, res_h, gain_h, wq_h, qscale_h,
     ns_o, out_o,
     gate, up, signs, dscale, res, gain1, qscale, wd, wq, gain,
     send1, recv1, recvr, resf, send2, recv2, lhsf, lhs, send3, recv3, send4, recv4, rowsf, lhs2,
-    sq, proj, send5, recv5,
+    sq, proj, early, send5, recv5,
     in_sem, wd_sem, wq_sem, s1, r1, sr, rr, s2, r2, s3, r3, s4, r4, s5, r5,
 ):
     h = lax.axis_index("hid")
@@ -141,6 +141,8 @@
         def _():
             landed(full, sem)
 
+    L = FFl // KC
+
     def but_mine(count, first, step):
         def guarded(index):
             @pl.when(first + index != h)
@@ -163,12 +165,14 @@
     right = jnp.dot(stacked, order, preferred_element_type=F32)
     parts = butterfly([right[p * Rl:(p + 1) * Rl, :] for p in range(pieces)])
     for p in range(pieces):
+        c, w = p * W // L, p * W % L
         for m in range(M):
-            send1[m, :, p * W:(p + 1) * W] = parts[p][m * q:(m + 1) * q, :].astype(BF16)
+            send1[c, m, :, w:w + W] = parts[p][m * q:(m + 1) * q, :].astype(BF16)
 
     @pl.when(owner)
     def _():
-        recv1[h] = send1[mine]
+        for c in range(KC):
+            recv1[c, h] = send1[c, mine]
 
     small[3].wait()
 
@@ -180,9 +184,9 @@
     def _():
         pl.semaphore_wait(barrier, M + B - 1)
 
-    def copy1(m, a):
+    def copy1(c, m, a):
         return pltpu.make_async_remote_copy(
-            src_ref=send1.at[m], dst_ref=recv1.at[a], send_sem=s1.at[0], recv_sem=r1.at[0],
+            src_ref=send1.at[c, m], dst_ref=recv1.at[c, a], send_sem=s1.at[0], recv_sem=r1.at[c],
             device_id={"hid": lo + m}, device_id_type=MESH,
         )
 
@@ -194,7 +198,20 @@
             device_id={"hid": home}, device_id_type=MESH,
         )
 
-    but_mine(M, lo, lambda m: copy1(m, h).start())
+    late = lax.div(h, (A + 1) // 2)
+
+    def far_first(step):
+        def guarded(index):
+            m = late * index + (1 - late) * (M - 1 - index)
+
+            @pl.when(lo + m != h)
+            def _():
+                step(m)
+
+        each(M, guarded)
+
+    for c in range(KC):
+        far_first(lambda m, c=c: copy1(c, m, h).start())
 
     @pl.when(home != h)
     def _():
@@ -208,36 +225,37 @@
         copy.wait()
     gain[...] = gain1[...].astype(F32).reshape(1, -1)
 
-    def copy2(t):
+    def copy2(c, t):
         peer = lax.rem(me + t, N)
         d = lax.div(peer, B)
         e = lax.rem(peer, B)
         return pltpu.make_async_remote_copy(
-            src_ref=send2.at[d], dst_ref=recv2.at[mine * B + r], send_sem=s2.at[e],
-            recv_sem=r2.at[0], device_id={"hid": d, "row": e},
+            src_ref=send2.at[c, d], dst_ref=recv2.at[c, mine * B + r], send_sem=s2.at[e],
+            recv_sem=r2.at[c], device_id={"hid": d, "row": e},
             device_id_type=MESH,
         )
 
     @pl.when(owner)
     def _():
-        landed(recv1.at[pl.ds(0, A - 1)], r1.at[0])
-        V = min(FFl, 512)
-        for c in range(0, FFl, V):
-            mixed = butterfly([recv1[a, :, c:c + V].astype(F32) for a in range(A)])
-            for a in range(A):
-                send2[a, :, c:c + V] = (mixed[a] * (1.0 / math.sqrt(FFl * A))).astype(BF16)
-        each(N, lambda t: copy2(t).start(), 1)
-        recv2[mine * B + r] = send2[h]
-
-    all_landed(recv2, recv2.at[pl.ds(0, M * B - 1)], r2.at[0])
+        V = min(L, 512)
+        for c in range(KC):
+            landed(recv1.at[c, pl.ds(0, A - 1)], r1.at[c])
+            for n in range(0, L, V):
+                mixed = butterfly([recv1[c, a, :, n:n + V].astype(F32) for a in range(A)])
+                for a in range(A):
+                    send2[c, a, :, n:n + V] = (mixed[a] * (1.0 / math.sqrt(FFl * A))).astype(BF16)
+            each(N, lambda t, c=c: copy2(c, t).start(), 1)
+            recv2[c, mine * B + r] = send2[c, h]
 
     for j in range(J):
         wq_copy(j).start(priority=1)
-    for b in range(B):
-        for m in range(M):
-            row = b * Rl + m * q
-            lhsf[row:row + q, :] = recv2[m * B + b].astype(F32)
-    lhs[...] = lhsf[...].astype(BF16)
+    def gather(c):
+        all_landed(recv2.at[c], recv2.at[c, pl.ds(0, M * B - 1)], r2.at[c])
+        for b in range(B):
+            for m in range(M):
+                row = b * Rl + m * q
+                lhsf[row:row + q, :] = recv2[c, m * B + b].astype(F32)
+        lhs[:, c * L:(c + 1) * L] = lhsf[...].astype(BF16)
 
     def copy3(m, a, j):
         return pltpu.make_async_remote_copy(
@@ -254,20 +272,44 @@
 
     tile = tile_of(C, 512)
 
+    def product(j, n, c, count):
+        return jnp.dot(
+            lhs[:, c * L:(c + count) * L], wd[j, c * L:(c + count) * L, n:n + tile],
+            preferred_element_type=F32,
+        )
+
+    def send_sums(j):
+        far_first(lambda m: copy3(m, h, j).start())
+
+        @pl.when(owner)
+        def _():
+            recv3[j, h] = send3[j, mine]
+
+    def put(j, n, part):
+        for m in range(M):
+            send3[j, m, :, n:n + tile] = part[m * T:(m + 1) * T, :].astype(BF16)
+
+    def first_step(j):
+        wd_copy(j).wait()
+        for n in range(0, C, tile):
+            early[j, :, n:n + tile] = product(j, n, 0, 1)
+
+    def second_step(j):
+        for n in range(0, C, tile):
+            put(j, n, early[j, :, n:n + tile] + product(j, n, 1, KC - 1))
+        send_sums(j)
+
     def down_step(j):
         wd_copy(j).wait()
         for n in range(0, C, tile):
-            part = jnp.dot(lhs[...], wd[j, :, n:n + tile], preferred_element_type=F32)
-            for m in range(M):
-                send3[j, m, :, n:n + tile] = part[m * T:(m + 1) * T, :].astype(BF16)
-
-        but_mine(M, lo, lambda m: copy3(m, h, j).start())
-
-        @pl.when(owner)
-        def _():
-            recv3[j, h] = send3[j, mine]
-
-    loop(J, down_step)
+            put(j, n, product(j, n, 0, KC))
+        send_sums(j)
+
+    gather(0)
+    loop(E, first_step)
+    gather(1)
+    loop(E, second_step)
+    loop(J, down_step, E)
 
     def stream_step(j):
         landed(recv3.at[j, pl.ds(0, A - 1)], r3.at[j])
@@ -328,7 +370,7 @@
     each(B, lambda t: copy5(t).start(), 1)
     recv5[r] = send5[r]
 
-    all_landed(send1, send1.at[pl.ds(0, M - 1)], s1.at[0])
+    all_landed(send1, send1.at[:, pl.ds(0, M - 1)], s1.at[0])
     all_landed(send3, send3.at[:, pl.ds(0, M - 1)], s3.at[0])
 
     @pl.when(home != h)
@@ -341,7 +383,7 @@
         for e in range(B):
             @pl.when(r == e)
             def _(e=e):
-                landed(send2.at[pl.ds(0, A - 1)], s2.at[e])
+                landed(send2.at[:, pl.ds(0, A - 1)], s2.at[e])
 
             @pl.when(r != e)
             def _(e=e):
@@ -379,13 +421,16 @@
     S = res.shape[0]
     q = Rl // M
     T = R // M
-    J = 8 if Dl % (8 * 128) == 0 else 4
+    J = 4 if Dl % (4 * 128) == 0 else 4
     C = Dl // J
+    KC = 2
+    E = 1
+    L = FFl // KC
     any_spec = pl.BlockSpec(memory_space=pl.ANY)
     vmem_spec = pl.BlockSpec(memory_space=pltpu.VMEM)
     dma = pltpu.SemaphoreType.DMA
     call = pl.pallas_call(
-        functools.partial(kernel, A, B, J, M, lo, Dl * B),
+        functools.partial(kernel, A, B, J, KC, E, M, lo, Dl * B),
         out_shape=(pltpu.VMEM((S, Dl), BF16), pltpu.VMEM((Rl, Q), BF16)),
         in_specs=[any_spec] * 9,
         out_specs=(vmem_spec, vmem_spec),
@@ -400,13 +445,13 @@
             pltpu.VMEM((J, FFl, C), BF16),
             pltpu.VMEM((J, C, Q), BF16),
             pltpu.VMEM((1, Dl), F32),
-            pltpu.VMEM((M, q, FFl), BF16),
-            pltpu.VMEM((A, q, FFl), BF16),
+            pltpu.VMEM((KC, M, q, L), BF16),
+            pltpu.VMEM((KC, A, q, L), BF16),
             pltpu.VMEM((A // M, S, Dl), BF16),
             pltpu.VMEM((T, Dl), F32),
-            pltpu.VMEM((A, q, FFl), BF16),
-            pltpu.VMEM((M * B, q, FFl), BF16),
-            pltpu.VMEM((R, FFl), F32),
+            pltpu.VMEM((KC, A, q, L), BF16),
+            pltpu.VMEM((KC, M * B, q, L), BF16),
+            pltpu.VMEM((R, L), F32),
             pltpu.VMEM((R, FFl), BF16),
             pltpu.VMEM((J, M, T, C), BF16),
             pltpu.VMEM((J, A, T, C), BF16),
@@ -416,17 +461,18 @@
             pltpu.VMEM((R, C), BF16),
             pltpu.VMEM((R, 128), F32),
             pltpu.VMEM((R, Q), F32),
+            pltpu.VMEM((E, R, C), F32),
             pltpu.VMEM((B, Rl, Q + 128), F32),
             pltpu.VMEM((B, Rl, Q + 128), F32),
             dma((7,)),
             dma((J,)),
             dma((J,)),
             dma((1,)),
-            dma((1,)),
+            dma((KC,)),
             dma((1,)),
             dma((A // M,)),
             dma((B,)),
-            dma((1,)),
+            dma((KC,)),
             dma((1,)),
             dma((J,)),
             dma((1,)),

time: 29 us -> 28.1 us (0.969)
  Pallas kernels: 28.2 us -> 27.3 us
    pallas_call x1, Pallas kernels: 27.5 us -> 26.6 us  [body(): call(gate, up, signs.reshape(1, -1), wd, dscale.reshape(1, -1), res, gain...]
where the time goes in v3:
time: 28.1 us; the launch traced here: 27.9 us
  Pallas kernels  27.3 us (97%)
  between operations  0.64 us (2%)
    pallas_call x1, Pallas kernels, body(): call(gate, up, signs.reshape(1, -1), wd, dscale.reshape(1, -1), res, gain...  26.6 us
    pallas_call x1, Pallas kernels, body(): pl.pallas_call(hand_over, out_shape=(jax.ShapeDtypeStruct((S, Dl), BF16),...  0.64 us

profile of v3, /device:TPU:0, one launch (start us, length us, event | category | flops | bytes accessed | tf_op | source)
XLA Modules:
  0.0 27.9 jit_solution(174366942334384387)
XLA Ops:
  0.6 26.6 %shard_map.104 = (bf16[2,4096]{1,0:T(2,128)(2,1)S(1)}, bf16[8,2304]{1,0:T(8,128)(2,1)S(1)}) custom-call(bf16[8,4096]{1,0:T(8,128)(2,1)} %gate_h.1, bf16[8,4096]{1,0:T(8,128)(2,1)} %up_h.1, s32[1,4096]{1,0:T(1,128)} %bitcast.2, bf16[4096,4096]{1,0:T(8,128)(2,1)} %wd_h.1, s32[1,4096]{1,0:T(1,128)} %bitcast.3, bf16[2,4096]{1,0:T(2,128)(2,1)} %res_h.1, ...), custom_call_target="tpu_custom_call" | custom-call | tf_op jit(solution)/shard_map/pallas_call | solution.py:487
  27.3 0.6 %shard_map.105 = (bf16[2,4096]{1,0:T(2,128)(2,1)}, bf16[8,2304]{1,0:T(8,128)(2,1)}) custom-call(bf16[2,4096]{1,0:T(2,128)(2,1)S(1)} %get-tuple-element.4.ns, bf16[8,2304]{1,0:T(8,128)(2,1)S(1)} %get-tuple-element.5.out), custom_call_target="tpu_custom_call" | custom-call | tf_op jit(solution)/shard_map/pallas_call | solution.py:491

commit v4 on v3

--- a/solution.py
+++ b/solution.py
@@ -67,7 +67,7 @@
 
 
 def kernel(
-    A, B, J, KC, E, M, lo, width_total,
+    A, B, J, KC, pairs, M, lo, width_total,
     gate_h, up_h, signs_h, wd_h, dscale_h, res_h, gain_h, wq_h, qscale_h,
     ns_o, out_o,
     gate, up, signs, dscale, res, gain1, qscale, wd, wq, gain,
@@ -88,7 +88,7 @@
     T = R // M
     G = A // M
     C = wd.shape[2]
-    Q = wq.shape[2]
+    Q = wq.shape[1]
 
     small = [
         pltpu.make_async_copy(src, dst, in_sem.at[k])
@@ -123,7 +123,7 @@
 
     def wq_copy(j):
         return pltpu.make_async_copy(
-            wq_h.at[pl.ds(pl.multiple_of(j * C, C), C), :], wq.at[j], wq_sem.at[j]
+            wq_h.at[pl.ds(pl.multiple_of(j * C, C), C), :], wq.at[pl.ds(pl.multiple_of(j * C, C), C), :], wq_sem.at[j]
         )
 
     for j in range(J):
@@ -225,8 +225,11 @@
         copy.wait()
     gain[...] = gain1[...].astype(F32).reshape(1, -1)
 
+    def far(index, count):
+        return late * index + (1 - late) * (count - 1 - index)
+
     def copy2(c, t):
-        peer = lax.rem(me + t, N)
+        peer = far(t, N)
         d = lax.div(peer, B)
         e = lax.rem(peer, B)
         return pltpu.make_async_remote_copy(
@@ -244,7 +247,13 @@
                 mixed = butterfly([recv1[c, a, :, n:n + V].astype(F32) for a in range(A)])
                 for a in range(A):
                     send2[c, a, :, n:n + V] = (mixed[a] * (1.0 / math.sqrt(FFl * A))).astype(BF16)
-            each(N, lambda t, c=c: copy2(c, t).start(), 1)
+
+            def send_rotated(t, c=c):
+                @pl.when(far(t, N) != me)
+                def _():
+                    copy2(c, t).start()
+
+            each(N, send_rotated)
             recv2[c, mine * B + r] = send2[c, h]
 
     for j in range(J):
@@ -257,18 +266,22 @@
                 lhsf[row:row + q, :] = recv2[c, m * B + b].astype(F32)
         lhs[:, c * L:(c + 1) * L] = lhsf[...].astype(BF16)
 
-    def copy3(m, a, j):
+    def copy3(m, a, unit, width, g):
         return pltpu.make_async_remote_copy(
-            src_ref=send3.at[j, m], dst_ref=recv3.at[j, a], send_sem=s3.at[0],
-            recv_sem=r3.at[j], device_id={"hid": lo + m}, device_id_type=MESH,
-        )
-
-    def copy4(t, m, j):
-        d = lax.rem(h + t, A)
+            src_ref=send3.at[m, pl.ds(unit, width)], dst_ref=recv3.at[a, pl.ds(unit, width)],
+            send_sem=s3.at[0], recv_sem=r3.at[g], device_id={"hid": lo + m}, device_id_type=MESH,
+        )
+
+    def copy4(t, m, unit, width, g):
+        d = far(t, A)
         return pltpu.make_async_remote_copy(
-            src_ref=send4.at[j], dst_ref=recv4.at[j, m], send_sem=s4.at[0],
-            recv_sem=r4.at[j], device_id={"hid": d}, device_id_type=MESH,
-        )
+            src_ref=send4.at[pl.ds(unit, width)], dst_ref=recv4.at[m, pl.ds(unit, width)],
+            send_sem=s4.at[0], recv_sem=r4.at[g], device_id={"hid": d}, device_id_type=MESH,
+        )
+
+    def groups(step, start=0):
+        loop(pairs, lambda g: step(2 * g, 2, g), start)
+        loop(pairs + 2, lambda g: step(pairs + g, 1, g), pairs)
 
     tile = tile_of(C, 512)
 
@@ -278,50 +291,62 @@
             preferred_element_type=F32,
         )
 
-    def send_sums(j):
-        far_first(lambda m: copy3(m, h, j).start())
+    def send_sums(unit, width, g):
+        far_first(lambda m: copy3(m, h, unit, width, g).start())
 
         @pl.when(owner)
         def _():
-            recv3[j, h] = send3[j, mine]
+            recv3[h, pl.ds(unit, width)] = send3[mine, pl.ds(unit, width)]
 
     def put(j, n, part):
         for m in range(M):
-            send3[j, m, :, n:n + tile] = part[m * T:(m + 1) * T, :].astype(BF16)
-
-    def first_step(j):
-        wd_copy(j).wait()
-        for n in range(0, C, tile):
-            early[j, :, n:n + tile] = product(j, n, 0, 1)
-
-    def second_step(j):
-        for n in range(0, C, tile):
-            put(j, n, early[j, :, n:n + tile] + product(j, n, 1, KC - 1))
-        send_sums(j)
-
-    def down_step(j):
-        wd_copy(j).wait()
-        for n in range(0, C, tile):
-            put(j, n, product(j, n, 0, KC))
-        send_sums(j)
+            send3[m, j, :, n:n + tile] = part[m * T:(m + 1) * T, :].astype(BF16)
+
+    def first_step():
+        for j in range(2):
+            wd_copy(j).wait()
+            for n in range(0, C, tile):
+                early[j, :, n:n + tile] = product(j, n, 0, 1)
+
+    def second_step():
+        for j in range(2):
+            for n in range(0, C, tile):
+                put(j, n, early[j, :, n:n + tile] + product(j, n, 1, KC - 1))
+        send_sums(0, 2, 0)
+
+    def down_step(unit, width, g):
+        for u in range(width):
+            wd_copy(unit + u).wait()
+        for u in range(width):
+            for n in range(0, C, tile):
+                put(unit + u, n, product(unit + u, n, 0, KC))
+        send_sums(unit, width, g)
 
     gather(0)
-    loop(E, first_step)
+    first_step()
     gather(1)
-    loop(E, second_step)
-    loop(J, down_step, E)
-
-    def stream_step(j):
-        landed(recv3.at[j, pl.ds(0, A - 1)], r3.at[j])
-        total = recv3[j, 0].astype(F32)
-        for a in range(1, A):
-            total = total + recv3[j, a].astype(F32)
-        columns = pl.ds(pl.multiple_of(j * C, C), C)
-        total = total * (dscale[:, columns].astype(F32) * 2.0 ** (-23))
-        stream = (resf[:, columns] + total).astype(BF16)
-        send4[j] = stream
-        recv4[j, mine] = stream
-        each(A, lambda t: copy4(t, mine, j).start(), 1)
+    second_step()
+    groups(down_step, 1)
+
+    def stream_step(unit, width, g):
+        landed(recv3.at[pl.ds(0, A - 1), pl.ds(unit, width)], r3.at[g])
+        for u in range(width):
+            j = unit + u
+            total = recv3[0, j].astype(F32)
+            for a in range(1, A):
+                total = total + recv3[a, j].astype(F32)
+            columns = pl.ds(pl.multiple_of(j * C, C), C)
+            total = total * (dscale[:, columns].astype(F32) * 2.0 ** (-23))
+            stream = (resf[:, columns] + total).astype(BF16)
+            send4[j] = stream
+            recv4[mine, j] = stream
+
+        def send_stream(t):
+            @pl.when(far(t, A) != h)
+            def _():
+                copy4(t, mine, unit, width, g).start()
+
+        each(A, send_stream)
 
     @pl.when(owner)
     def _():
@@ -331,31 +356,35 @@
                 copyr(g).wait_recv()
         for g in range(G):
             resf[g * S:(g + 1) * S, :] = recvr[g].astype(F32)
-        loop(J, stream_step)
+        groups(stream_step)
 
     sq[...] = jnp.zeros_like(sq)
     proj[...] = jnp.zeros_like(proj)
     tile_q = tile_of(Q, 768)
 
-    def project_step(j):
-        all_landed(recv4.at[j], recv4.at[j, pl.ds(0, M - 1)], r4.at[j])
-        wq_copy(j).wait()
-        for m in range(M):
-            rowsf[m * T:(m + 1) * T, :] = recv4[j, m].astype(F32)
-        wide = rowsf[...]
-        columns = pl.ds(pl.multiple_of(j * C, C), C)
+    def project_step(unit, width, g):
+        all_landed(
+            recv4.at[:, pl.ds(unit, width)], recv4.at[pl.ds(0, M - 1), pl.ds(unit, width)], r4.at[g]
+        )
+        for u in range(width):
+            wq_copy(unit + u).wait()
+            for m in range(M):
+                rowsf[m * T:(m + 1) * T, u * C:(u + 1) * C] = recv4[m, unit + u].astype(F32)
+        span = width * C
+        wide = rowsf[:, :span]
+        columns = pl.ds(pl.multiple_of(unit * C, C), span)
         for a in range(A):
             @pl.when(h == a)
-            def _():
-                ns_o[:, columns] = rowsf[a * S:(a + 1) * S, :].astype(BF16)
-        lhs2[...] = (wide * gain[:, columns]).astype(BF16)
+            def _(a=a):
+                ns_o[:, columns] = rowsf[a * S:(a + 1) * S, :span].astype(BF16)
+        lhs2[:, :span] = (wide * gain[:, columns]).astype(BF16)
         sq[...] += jnp.sum(wide * wide, axis=1, keepdims=True)
         for n in range(0, Q, tile_q):
             proj[:, n:n + tile_q] += jnp.dot(
-                lhs2[...], wq[j, :, n:n + tile_q], preferred_element_type=F32
+                lhs2[:, :span], wq[columns, n:n + tile_q], preferred_element_type=F32
             )
 
-    loop(J, project_step)
+    groups(project_step)
 
     def copy5(t):
         d = lax.rem(r + t, B)
@@ -371,7 +400,7 @@
     recv5[r] = send5[r]
 
     all_landed(send1, send1.at[:, pl.ds(0, M - 1)], s1.at[0])
-    all_landed(send3, send3.at[:, pl.ds(0, M - 1)], s3.at[0])
+    all_landed(send3, send3.at[pl.ds(0, M - 1)], s3.at[0])
 
     @pl.when(home != h)
     def _():
@@ -379,7 +408,7 @@
 
     @pl.when(owner)
     def _():
-        landed(recv3.at[:, pl.ds(0, A - 1)], s4.at[0])
+        landed(recv3.at[pl.ds(0, A - 1)], s4.at[0])
         for e in range(B):
             @pl.when(r == e)
             def _(e=e):
@@ -421,16 +450,15 @@
     S = res.shape[0]
     q = Rl // M
     T = R // M
-    J = 4 if Dl % (4 * 128) == 0 else 4
+    J = 8 if Dl % (8 * 128) == 0 else 4
     C = Dl // J
     KC = 2
-    E = 1
     L = FFl // KC
     any_spec = pl.BlockSpec(memory_space=pl.ANY)
     vmem_spec = pl.BlockSpec(memory_space=pltpu.VMEM)
     dma = pltpu.SemaphoreType.DMA
     call = pl.pallas_call(
-        functools.partial(kernel, A, B, J, KC, E, M, lo, Dl * B),
+        functools.partial(kernel, A, B, J, KC, J // 2 - 1, M, lo, Dl * B),
         out_shape=(pltpu.VMEM((S, Dl), BF16), pltpu.VMEM((Rl, Q), BF16)),
         in_specs=[any_spec] * 9,
         out_specs=(vmem_spec, vmem_spec),
@@ -443,7 +471,7 @@
             pltpu.VMEM((Dl,), BF16),
             pltpu.VMEM((Q,), jnp.int32),
             pltpu.VMEM((J, FFl, C), BF16),
-            pltpu.VMEM((J, C, Q), BF16),
+            pltpu.VMEM((Dl, Q), BF16),
             pltpu.VMEM((1, Dl), F32),
             pltpu.VMEM((KC, M, q, L), BF16),
             pltpu.VMEM((KC, A, q, L), BF16),
@@ -453,15 +481,15 @@
             pltpu.VMEM((KC, M * B, q, L), BF16),
             pltpu.VMEM((R, L), F32),
             pltpu.VMEM((R, FFl), BF16),
-            pltpu.VMEM((J, M, T, C), BF16),
-            pltpu.VMEM((J, A, T, C), BF16),
+            pltpu.VMEM((M, J, T, C), BF16),
+            pltpu.VMEM((A, J, T, C), BF16),
             pltpu.VMEM((J, T, C), BF16),
-            pltpu.VMEM((J, M, T, C), BF16),
-            pltpu.VMEM((R, C), F32),
-            pltpu.VMEM((R, C), BF16),
+            pltpu.VMEM((M, J, T, C), BF16),
+            pltpu.VMEM((R, 2 * C), F32),
+            pltpu.VMEM((R, 2 * C), BF16),
             pltpu.VMEM((R, 128), F32),
             pltpu.VMEM((R, Q), F32),
-            pltpu.VMEM((E, R, C), F32),
+            pltpu.VMEM((2, R, C), F32),
             pltpu.VMEM((B, Rl, Q + 128), F32),
             pltpu.VMEM((B, Rl, Q + 128), F32),
             dma((7,)),
@@ -474,9 +502,9 @@
             dma((B,)),
             dma((KC,)),
             dma((1,)),
-            dma((J,)),
+            dma((J // 2 + 1,)),
             dma((1,)),
-            dma((J,)),
+            dma((J // 2 + 1,)),
             dma((B - 1,)),
             dma((B - 1,)),
         ],

time: 28.1 us -> 27.9 us (level)
  no operation moved by 1% of the time
where the time goes in v4:
time: 27.9 us; the launch traced here: 27.7 us
  Pallas kernels  27.1 us (97%)
  between operations  0.64 us (2%)
    pallas_call x1, Pallas kernels, body(): call(gate, up, signs.reshape(1, -1), wd, dscale.reshape(1, -1), res, gain...  26.5 us
    pallas_call x1, Pallas kernels, body(): pl.pallas_call(hand_over, out_shape=(jax.ShapeDtypeStruct((S, Dl), BF16),...  0.64 us

profile of v4, /device:TPU:0, one launch (start us, length us, event | category | flops | bytes accessed | tf_op | source)
XLA Modules:
  0.0 27.7 jit_solution(14044846562025721516)
XLA Ops:
  0.6 26.5 %shard_map.104 = (bf16[2,4096]{1,0:T(2,128)(2,1)S(1)}, bf16[8,2304]{1,0:T(8,128)(2,1)S(1)}) custom-call(bf16[8,4096]{1,0:T(8,128)(2,1)} %gate_h.1, bf16[8,4096]{1,0:T(8,128)(2,1)} %up_h.1, s32[1,4096]{1,0:T(1,128)} %bitcast.2, bf16[4096,4096]{1,0:T(8,128)(2,1)} %wd_h.1, s32[1,4096]{1,0:T(1,128)} %bitcast.3, bf16[2,4096]{1,0:T(2,128)(2,1)} %res_h.1, ...), custom_call_target="tpu_custom_call" | custom-call | tf_op jit(solution)/shard_map/pallas_call | solution.py:515
  27.1 0.6 %shard_map.105 = (bf16[2,4096]{1,0:T(2,128)(2,1)}, bf16[8,2304]{1,0:T(8,128)(2,1)}) custom-call(bf16[2,4096]{1,0:T(2,128)(2,1)S(1)} %get-tuple-element.4.ns, bf16[8,2304]{1,0:T(8,128)(2,1)S(1)} %get-tuple-element.5.out), custom_call_target="tpu_custom_call" | custom-call | tf_op jit(solution)/shard_map/pallas_call | solution.py:519
